TPU v7x, 256 devices: a whole 4x4x8 slice. The times are simulated.
256 devices in a mesh: seq: 32 (over y, z), head: 8 (over x, core).
Axes of the slice: x: 4, y: 4, z: 8, core: 2. Of those that a mesh axis runs over, the one named last changes fastest.
Arguments:
- query: bfloat16 [16384, 2048], P('seq', 'head'), may hold values from -6 to 6
- keys: bfloat16 [16384, 2048], P('seq', 'head'), may hold values from -6 to 6
- values: bfloat16 [16384, 4096], P('seq', 'head'), may hold values from -6 to 6
- gate_logit: float32 [16384, 32], P('seq', 'head'), may hold values from -17 to 1.5
- beta_logit: float32 [16384, 32], P('seq', 'head'), may hold values from -9 to 6
- decay_rate: float32 [32], P('head'), may hold values from 0.5 to 8
- norm_gain: float32 [128], replicated, may hold values from 0.1 to 1.9
- gate_z: bfloat16 [16384, 4096], P('seq', 'head'), may hold values from -6 to 6
- out_weight: bfloat16 [4096, 2048], P('head'), may hold values from -0.09375 to 0.09375
Outputs:
- mixed: bfloat16 [16384, 2048], P(('seq', 'head'))
All inputs are finite; a program needn't handle non-finite values.
Results may differ from a plain program's by a relative error of at most 0.014.
Values may be sent and summed in bfloat16 or wider, within the bound.
A program may use at most 128 MiB of HBM per device.

v0:
```python
import jax
import jax.numpy as jnp
from jax import lax
from jax.sharding import PartitionSpec as P

DK = 128
DV = 128
SPAN = 64


def passed_along(shard, axis, by):
    size = lax.axis_size(axis)
    pairs = [(i, i + by) for i in range(size) if 0 <= i + by < size]
    return lax.ppermute(shard, axis, pairs)


def unit_norm(values_in):
    return values_in * lax.rsqrt(jnp.sum(values_in * values_in, axis=-1, keepdims=True) + 1e-06)


def block_terms(query, keys, values, logdecay, beta):
    highest = lax.Precision.HIGHEST
    size = logdecay.shape[-1]
    width = keys.shape[-1]
    cumul = jnp.cumsum(logdecay, axis=-1)
    differ = cumul[..., :, None] - cumul[..., None, :]
    row_ids = lax.broadcasted_iota(jnp.int32, (size, size), 0)
    col_ids = lax.broadcasted_iota(jnp.int32, (size, size), 1)
    inclusive = col_ids <= row_ids
    strict = col_ids < row_ids
    ratio = jnp.where(inclusive, jnp.exp(jnp.where(inclusive, differ, 0.0)), 0.0)
    key_key = jnp.einsum("...te,...se->...ts", keys, keys, precision=highest)
    query_key = jnp.einsum("...te,...se->...ts", query, keys, precision=highest)
    lower = jnp.where(strict, beta[..., :, None] * ratio * key_key, 0.0) + jnp.eye(
        size, dtype=jnp.float32
    )
    rhs_values = beta[..., None] * values
    rhs_keys = (beta * jnp.exp(cumul))[..., None] * keys
    update = lax.linalg.triangular_solve(
        lower, rhs_values, left_side=True, lower=True, unit_diagonal=True
    )
    weights = lax.linalg.triangular_solve(
        lower, rhs_keys, left_side=True, lower=True, unit_diagonal=True
    )
    mixing = ratio * query_key
    decayed_query = jnp.exp(cumul)[..., None] * query
    key_end = jnp.exp(cumul[..., -1:] - cumul)[..., None] * keys
    transit = jnp.exp(cumul[..., -1])[..., None, None] * jnp.eye(width, dtype=jnp.float32)
    transit = transit - jnp.einsum("...se,...sf->...ef", key_end, weights, precision=highest)
    inject = jnp.einsum("...se,...sf->...ef", key_end, update, precision=highest)
    return (update, weights, mixing, decayed_query, transit, inject)


def run_blocks(terms, start):
    highest = lax.Precision.HIGHEST

    def advance(state, item):
        update, weights, mixing, decayed_query, transit, inject = item
        resid = update - jnp.einsum("...ce,...ef->...cf", weights, state, precision=highest)
        result = jnp.einsum("...ce,...ef->...cf", decayed_query, state, precision=highest)
        result = result + jnp.einsum("...ts,...sf->...tf", mixing, resid, precision=highest)
        state = jnp.einsum("...ef,...fg->...eg", transit, state, precision=highest) + inject
        return (state, result)

    return lax.scan(advance, start, terms)


def matmul_heads(left, right):
    return jnp.einsum("hef,hfg->heg", left, right, precision=lax.Precision.HIGHEST)


def on_device(
    query, keys, values, gate_logit, beta_logit, decay_rate, norm_gain, gate_z, out_weight
):
    tok_rows = query.shape[0]
    local_heads = values.shape[1] // DV
    key_heads = query.shape[1] // DK
    blocks = tok_rows // SPAN

    def to_blocks(array, width):
        return array.reshape(blocks, SPAN, local_heads, width).transpose(0, 2, 1, 3)

    qn = jnp.repeat(
        unit_norm(query.astype(jnp.float32).reshape(tok_rows, key_heads, DK)), 2, axis=1
    )
    kn = jnp.repeat(unit_norm(keys.astype(jnp.float32).reshape(tok_rows, key_heads, DK)), 2, axis=1)
    vals = values.astype(jnp.float32).reshape(tok_rows, local_heads, DV)
    logdecay = -decay_rate[None, :] * jax.nn.softplus(gate_logit)
    beta = jax.nn.sigmoid(beta_logit)
    terms = block_terms(
        to_blocks(qn, DK),
        to_blocks(kn, DK),
        to_blocks(vals, DV),
        logdecay.reshape(blocks, SPAN, local_heads).transpose(0, 2, 1),
        beta.reshape(blocks, SPAN, local_heads).transpose(0, 2, 1),
    )
    ident = jnp.broadcast_to(jnp.eye(DK, dtype=jnp.float32), (local_heads, DK, DK))
    zeros = jnp.zeros((local_heads, DK, DV), jnp.float32)

    def compose(carry, item):
        transit, inject = item
        return ((matmul_heads(transit, carry[0]), matmul_heads(transit, carry[1]) + inject), None)

    (shard_transit, shard_inject), unused = lax.scan(compose, (ident, zeros), (terms[4], terms[5]))

    def relay(step, carry):
        ending = matmul_heads(shard_transit, carry) + shard_inject
        return passed_along(ending, "seq", 1)

    start = lax.fori_loop(0, lax.axis_size("seq") - 1, relay, zeros)
    final, outs = run_blocks(terms, start)
    core = outs.transpose(0, 2, 1, 3).reshape(tok_rows, local_heads, DV)
    gate = jax.nn.silu(gate_z.astype(jnp.float32).reshape(tok_rows, local_heads, DV))
    scale = lax.rsqrt(jnp.mean(core * core, axis=-1, keepdims=True) + 1e-06)
    gated = (
        (core * scale * norm_gain * gate).astype(jnp.bfloat16).reshape(tok_rows, local_heads * DV)
    )
    rows = lax.all_to_all(gated, "head", split_axis=0, concat_axis=1, tiled=True)
    mixed = jnp.dot(
        rows,
        lax.all_gather(out_weight, "head", axis=0, tiled=True),
        preferred_element_type=jnp.float32,
    )
    return mixed.astype(jnp.bfloat16)


def solution(mesh):
    return jax.shard_map(
        on_device,
        mesh=mesh,
        in_specs=(
            P("seq", "head"),
            P("seq", "head"),
            P("seq", "head"),
            P("seq", "head"),
            P("seq", "head"),
            P("head"),
            P(),
            P("seq", "head"),
            P("head", None),
        ),
        out_specs=P(("seq", "head"), None),
        check_vma=False,
    )
```

profile of v0, /device:TPU:24, one launch (start us, length us, event | category | flops | bytes accessed | tf_op | source)
XLA Modules:
  0.0 647.6 jit_solution(6673752401664360787)
XLA Ops:
  14.6 157.3 %custom-call.5 = f32[8,4,1,64,64]{3,4,2,1,0:T(8,128)S(1)} custom-call(f32[8,4,1,64,64]{4,3,2,1,0:T(8,128)S(1)} %fusion.30), custom_call_target="InvertDiagBlocksLowerTriangular" | custom-call | tf_op jit(solution)/shard_map/triangular_solve/custom-call.1 | solution.py:42
  192.2 14.6 %while.37 = (s32[]{:T(128)}, f32[4,128,128]{2,1,0:T(8,128)S(1)}, f32[4,128,128]{2,1,0:T(8,128)S(1)}, f32[8,4,128,128]{3,2,1,0:T(8,128)S(1)}, f32[8,4,128,128]{3,2,1,0:T(8,128)}, /*index=5*/s32[]{:T(128)}, s32[]{:T(128)}) while((s32[]{:T(128)}, f32[4,128,128]{2,1,0:T(8,128)S(1)}, f32[4,128,128]{2,1,0:T(8,128)S(1)}, ...), condition=%wide.region_3.5_spmd.clone, body=%wide.region_2.0_spmd.clone.sunk | while | flops 201457664 | bytes 2884699 | solution.py:104
  206.8 359.6 %while.35 = (s32[]{:T(128)}, f32[4,128,128]{2,1,0:T(8,128)S(1)}, f32[4,128,128]{2,1,0:T(8,128)S(1)}, f32[4,128,128]{2,1,0:T(8,128)S(1)}, s32[]{:T(128)}) while((s32[]{:T(128)}, f32[4,128,128]{2,1,0:T(8,128)S(1)}, f32[4,128,128]{2,1,0:T(8,128)S(1)}, f32[4,128,128]{2,1,0:T(8,128)S(1)}, s32[]{:T(128)}) %tuple.62), condition=%wide.region_5.7_spmd, body=%wide.region_4.6_spmd.sunk | while | flops 100728832 | bytes 2097253 | solution.py:110
  211.1 10.4 %collective-permute-done = f32[4,128,128]{2,1,0:T(8,128)S(1)} collective-permute-done((f32[4,128,128]{2,1,0:T(8,128)S(1)}, f32[4,128,128]{2,1,0:T(8,128)S(1)}, u32[]{:S(2)}, u32[]{:S(2)}) %collective-permute-start) | collective-permute-done | bytes 262176 | tf_op jit(solution)/shard_map/while/body/eval_jaxpr/ppermute | solution.py:14
  223.8 9.6 %collective-permute-done = f32[4,128,128]{2,1,0:T(8,128)S(1)} collective-permute-done((f32[4,128,128]{2,1,0:T(8,128)S(1)}, f32[4,128,128]{2,1,0:T(8,128)S(1)}, u32[]{:S(2)}, u32[]{:S(2)}) %collective-permute-start) | collective-permute-done | bytes 262176 | tf_op jit(solution)/shard_map/while/body/eval_jaxpr/ppermute | solution.py:14
  235.7 8.6 %collective-permute-done = f32[4,128,128]{2,1,0:T(8,128)S(1)} collective-permute-done((f32[4,128,128]{2,1,0:T(8,128)S(1)}, f32[4,128,128]{2,1,0:T(8,128)S(1)}, u32[]{:S(2)}, u32[]{:S(2)}) %collective-permute-start) | collective-permute-done | bytes 262176 | tf_op jit(solution)/shard_map/while/body/eval_jaxpr/ppermute | solution.py:14
  257.5 8.4 %collective-permute-done = f32[4,128,128]{2,1,0:T(8,128)S(1)} collective-permute-done((f32[4,128,128]{2,1,0:T(8,128)S(1)}, f32[4,128,128]{2,1,0:T(8,128)S(1)}, u32[]{:S(2)}, u32[]{:S(2)}) %collective-permute-start) | collective-permute-done | bytes 262176 | tf_op jit(solution)/shard_map/while/body/eval_jaxpr/ppermute | solution.py:14
  279.0 8.5 %collective-permute-done = f32[4,128,128]{2,1,0:T(8,128)S(1)} collective-permute-done((f32[4,128,128]{2,1,0:T(8,128)S(1)}, f32[4,128,128]{2,1,0:T(8,128)S(1)}, u32[]{:S(2)}, u32[]{:S(2)}) %collective-permute-start) | collective-permute-done | bytes 262176 | tf_op jit(solution)/shard_map/while/body/eval_jaxpr/ppermute | solution.py:14
  289.9 9.6 %collective-permute-done = f32[4,128,128]{2,1,0:T(8,128)S(1)} collective-permute-done((f32[4,128,128]{2,1,0:T(8,128)S(1)}, f32[4,128,128]{2,1,0:T(8,128)S(1)}, u32[]{:S(2)}, u32[]{:S(2)}) %collective-permute-start) | collective-permute-done | bytes 262176 | tf_op jit(solution)/shard_map/while/body/eval_jaxpr/ppermute | solution.py:14
  301.8 10.8 %collective-permute-done = f32[4,128,128]{2,1,0:T(8,128)S(1)} collective-permute-done((f32[4,128,128]{2,1,0:T(8,128)S(1)}, f32[4,128,128]{2,1,0:T(8,128)S(1)}, u32[]{:S(2)}, u32[]{:S(2)}) %collective-permute-start) | collective-permute-done | bytes 262176 | tf_op jit(solution)/shard_map/while/body/eval_jaxpr/ppermute | solution.py:14
  315.0 10.5 %collective-permute-done = f32[4,128,128]{2,1,0:T(8,128)S(1)} collective-permute-done((f32[4,128,128]{2,1,0:T(8,128)S(1)}, f32[4,128,128]{2,1,0:T(8,128)S(1)}, u32[]{:S(2)}, u32[]{:S(2)}) %collective-permute-start) | collective-permute-done | bytes 262176 | tf_op jit(solution)/shard_map/while/body/eval_jaxpr/ppermute | solution.py:14
  327.9 9.7 %collective-permute-done = f32[4,128,128]{2,1,0:T(8,128)S(1)} collective-permute-done((f32[4,128,128]{2,1,0:T(8,128)S(1)}, f32[4,128,128]{2,1,0:T(8,128)S(1)}, u32[]{:S(2)}, u32[]{:S(2)}) %collective-permute-start) | collective-permute-done | bytes 262176 | tf_op jit(solution)/shard_map/while/body/eval_jaxpr/ppermute | solution.py:14
  339.9 8.8 %collective-permute-done = f32[4,128,128]{2,1,0:T(8,128)S(1)} collective-permute-done((f32[4,128,128]{2,1,0:T(8,128)S(1)}, f32[4,128,128]{2,1,0:T(8,128)S(1)}, u32[]{:S(2)}, u32[]{:S(2)}) %collective-permute-start) | collective-permute-done | bytes 262176 | tf_op jit(solution)/shard_map/while/body/eval_jaxpr/ppermute | solution.py:14
  394.2 9.5 %collective-permute-done = f32[4,128,128]{2,1,0:T(8,128)S(1)} collective-permute-done((f32[4,128,128]{2,1,0:T(8,128)S(1)}, f32[4,128,128]{2,1,0:T(8,128)S(1)}, u32[]{:S(2)}, u32[]{:S(2)}) %collective-permute-start) | collective-permute-done | bytes 262176 | tf_op jit(solution)/shard_map/while/body/eval_jaxpr/ppermute | solution.py:14
  406.0 10.7 %collective-permute-done = f32[4,128,128]{2,1,0:T(8,128)S(1)} collective-permute-done((f32[4,128,128]{2,1,0:T(8,128)S(1)}, f32[4,128,128]{2,1,0:T(8,128)S(1)}, u32[]{:S(2)}, u32[]{:S(2)}) %collective-permute-start) | collective-permute-done | bytes 262176 | tf_op jit(solution)/shard_map/while/body/eval_jaxpr/ppermute | solution.py:14
  419.1 10.6 %collective-permute-done = f32[4,128,128]{2,1,0:T(8,128)S(1)} collective-permute-done((f32[4,128,128]{2,1,0:T(8,128)S(1)}, f32[4,128,128]{2,1,0:T(8,128)S(1)}, u32[]{:S(2)}, u32[]{:S(2)}) %collective-permute-start) | collective-permute-done | bytes 262176 | tf_op jit(solution)/shard_map/while/body/eval_jaxpr/ppermute | solution.py:14
  432.1 9.8 %collective-permute-done = f32[4,128,128]{2,1,0:T(8,128)S(1)} collective-permute-done((f32[4,128,128]{2,1,0:T(8,128)S(1)}, f32[4,128,128]{2,1,0:T(8,128)S(1)}, u32[]{:S(2)}, u32[]{:S(2)}) %collective-permute-start) | collective-permute-done | bytes 262176 | tf_op jit(solution)/shard_map/while/body/eval_jaxpr/ppermute | solution.py:14
  444.2 8.9 %collective-permute-done = f32[4,128,128]{2,1,0:T(8,128)S(1)} collective-permute-done((f32[4,128,128]{2,1,0:T(8,128)S(1)}, f32[4,128,128]{2,1,0:T(8,128)S(1)}, u32[]{:S(2)}, u32[]{:S(2)}) %collective-permute-start) | collective-permute-done | bytes 262176 | tf_op jit(solution)/shard_map/while/body/eval_jaxpr/ppermute | solution.py:14
  498.6 9.4 %collective-permute-done = f32[4,128,128]{2,1,0:T(8,128)S(1)} collective-permute-done((f32[4,128,128]{2,1,0:T(8,128)S(1)}, f32[4,128,128]{2,1,0:T(8,128)S(1)}, u32[]{:S(2)}, u32[]{:S(2)}) %collective-permute-start) | collective-permute-done | bytes 262176 | tf_op jit(solution)/shard_map/while/body/eval_jaxpr/ppermute | solution.py:14
  510.3 10.6 %collective-permute-done = f32[4,128,128]{2,1,0:T(8,128)S(1)} collective-permute-done((f32[4,128,128]{2,1,0:T(8,128)S(1)}, f32[4,128,128]{2,1,0:T(8,128)S(1)}, u32[]{:S(2)}, u32[]{:S(2)}) %collective-permute-start) | collective-permute-done | bytes 262176 | tf_op jit(solution)/shard_map/while/body/eval_jaxpr/ppermute | solution.py:14
  523.3 10.7 %collective-permute-done = f32[4,128,128]{2,1,0:T(8,128)S(1)} collective-permute-done((f32[4,128,128]{2,1,0:T(8,128)S(1)}, f32[4,128,128]{2,1,0:T(8,128)S(1)}, u32[]{:S(2)}, u32[]{:S(2)}) %collective-permute-start) | collective-permute-done | bytes 262176 | tf_op jit(solution)/shard_map/while/body/eval_jaxpr/ppermute | solution.py:14
  566.4 46.7 %while.36 = (s32[]{:T(128)}, f32[4,128,128]{2,1,0:T(8,128)S(1)}, f32[8,4,64,128]{3,2,1,0:T(8,128)}, f32[8,4,128,128]{3,2,1,0:T(8,128)S(1)}, f32[8,4,128,128]{3,2...) while((s32[]{:T(128)}, f32[4,128,128]{2,1,0:T(8,128)S(1)}, ...), condition=%wide.region_8.10_spmd, body=%wide.region_7.9_spmd.sunk | while | flops 226623488 | bytes 3280485 | solution.py:65
  616.7 14.5 %all_to_all.19 = bf16[8,64,512]{2,1,0:T(8,128)(2,1)S(1)} all-to-all(bf16[8,64,512]{2,1,0:T(8,128)(2,1)S(1)} %bitcast.135), channel_id=1, replica_groups=mesh['seq'=32,'head'=8] {'head'}, dimensions={0} | all-to-all | bytes 1048576 | tf_op jit(solution)/shard_map/all_to_all | solution.py:118
  631.2 9.5 %convolution_convert_fusion = bf16[64,2048]{1,0:T(8,128)(2,1)} fusion(bf16[64,4096]{1,0:T(8,128)(2,1)S(1)} %bitcast.133, bf16[4096,2048]{1,0:T(8,128)(2,1)} %all-gather.2.cloned.1.call-done), kind=kOutput, calls=%fused_computation.31 | convolution fusion | flops 1073872896 | bytes 17563648 | tf_op jit(solution)/shard_map/dot_general | solution.py:119
  (219 shorter events, 275.8 us)
Async XLA Ops:
  6.5 624.7 %all-gather.2.cloned.1.call-start = ((), (), s32[]{:S(2)}) async-start(), calls=%async_computation.1 | async-start | bytes 18874368 | tf_op jit(solution)/shard_map/all_gather | solution.py:121
  207.2 14.2 %collective-permute-start = (f32[4,128,128]{2,1,0:T(8,128)S(1)}, f32[4,128,128]{2,1,0:T(8,128)S(1)}, u32[]{:S(2)}, u32[]{:S(2)}) collective-permute-start(f32[4,128,128]{2,1,0:T(8,128)S(1)} %convolution_add_fusion.7), channel_id=1, source_target_pairs={{0,8},{8,16},{16,24},{24,32},{32,40},{40,48},{48,56},{56,64},{64,7... | collective-permute-start | bytes 786440 | tf_op jit(solution)/shard_map/while/body/eval_jaxpr/ppermute | solution.py:14
  221.9 11.5 %collective-permute-start = (f32[4,128,128]{2,1,0:T(8,128)S(1)}, f32[4,128,128]{2,1,0:T(8,128)S(1)}, u32[]{:S(2)}, u32[]{:S(2)}) collective-permute-start(f32[4,128,128]{2,1,0:T(8,128)S(1)} %convolution_add_fusion.7), channel_id=1, source_target_pairs={{0,8},{8,16},{16,24},{24,32},{32,40},{40,48},{48,56},{56,64},{64,7... | collective-permute-start | bytes 786440 | tf_op jit(solution)/shard_map/while/body/eval_jaxpr/ppermute | solution.py:14
  233.8 10.6 %collective-permute-start = (f32[4,128,128]{2,1,0:T(8,128)S(1)}, f32[4,128,128]{2,1,0:T(8,128)S(1)}, u32[]{:S(2)}, u32[]{:S(2)}) collective-permute-start(f32[4,128,128]{2,1,0:T(8,128)S(1)} %convolution_add_fusion.7), channel_id=1, source_target_pairs={{0,8},{8,16},{16,24},{24,32},{32,40},{40,48},{48,56},{56,64},{64,7... | collective-permute-start | bytes 786440 | tf_op jit(solution)/shard_map/while/body/eval_jaxpr/ppermute | solution.py:14
  244.8 10.4 %collective-permute-start = (f32[4,128,128]{2,1,0:T(8,128)S(1)}, f32[4,128,128]{2,1,0:T(8,128)S(1)}, u32[]{:S(2)}, u32[]{:S(2)}) collective-permute-start(f32[4,128,128]{2,1,0:T(8,128)S(1)} %convolution_add_fusion.7), channel_id=1, source_target_pairs={{0,8},{8,16},{16,24},{24,32},{32,40},{40,48},{48,56},{56,64},{64,7... | collective-permute-start | bytes 786440 | tf_op jit(solution)/shard_map/while/body/eval_jaxpr/ppermute | solution.py:14
  255.5 10.4 %collective-permute-start = (f32[4,128,128]{2,1,0:T(8,128)S(1)}, f32[4,128,128]{2,1,0:T(8,128)S(1)}, u32[]{:S(2)}, u32[]{:S(2)}) collective-permute-start(f32[4,128,128]{2,1,0:T(8,128)S(1)} %convolution_add_fusion.7), channel_id=1, source_target_pairs={{0,8},{8,16},{16,24},{24,32},{32,40},{40,48},{48,56},{56,64},{64,7... | collective-permute-start | bytes 786440 | tf_op jit(solution)/shard_map/while/body/eval_jaxpr/ppermute | solution.py:14
  266.3 10.4 %collective-permute-start = (f32[4,128,128]{2,1,0:T(8,128)S(1)}, f32[4,128,128]{2,1,0:T(8,128)S(1)}, u32[]{:S(2)}, u32[]{:S(2)}) collective-permute-start(f32[4,128,128]{2,1,0:T(8,128)S(1)} %convolution_add_fusion.7), channel_id=1, source_target_pairs={{0,8},{8,16},{16,24},{24,32},{32,40},{40,48},{48,56},{56,64},{64,7... | collective-permute-start | bytes 786440 | tf_op jit(solution)/shard_map/while/body/eval_jaxpr/ppermute | solution.py:14
  277.1 10.5 %collective-permute-start = (f32[4,128,128]{2,1,0:T(8,128)S(1)}, f32[4,128,128]{2,1,0:T(8,128)S(1)}, u32[]{:S(2)}, u32[]{:S(2)}) collective-permute-start(f32[4,128,128]{2,1,0:T(8,128)S(1)} %convolution_add_fusion.7), channel_id=1, source_target_pairs={{0,8},{8,16},{16,24},{24,32},{32,40},{40,48},{48,56},{56,64},{64,7... | collective-permute-start | bytes 786440 | tf_op jit(solution)/shard_map/while/body/eval_jaxpr/ppermute | solution.py:14
  288.0 11.5 %collective-permute-start = (f32[4,128,128]{2,1,0:T(8,128)S(1)}, f32[4,128,128]{2,1,0:T(8,128)S(1)}, u32[]{:S(2)}, u32[]{:S(2)}) collective-permute-start(f32[4,128,128]{2,1,0:T(8,128)S(1)} %convolution_add_fusion.7), channel_id=1, source_target_pairs={{0,8},{8,16},{16,24},{24,32},{32,40},{40,48},{48,56},{56,64},{64,7... | collective-permute-start | bytes 786440 | tf_op jit(solution)/shard_map/while/body/eval_jaxpr/ppermute | solution.py:14
  299.9 12.8 %collective-permute-start = (f32[4,128,128]{2,1,0:T(8,128)S(1)}, f32[4,128,128]{2,1,0:T(8,128)S(1)}, u32[]{:S(2)}, u32[]{:S(2)}) collective-permute-start(f32[4,128,128]{2,1,0:T(8,128)S(1)} %convolution_add_fusion.7), channel_id=1, source_target_pairs={{0,8},{8,16},{16,24},{24,32},{32,40},{40,48},{48,56},{56,64},{64,7... | collective-permute-start | bytes 786440 | tf_op jit(solution)/shard_map/while/body/eval_jaxpr/ppermute | solution.py:14
  313.1 12.5 %collective-permute-start = (f32[4,128,128]{2,1,0:T(8,128)S(1)}, f32[4,128,128]{2,1,0:T(8,128)S(1)}, u32[]{:S(2)}, u32[]{:S(2)}) collective-permute-start(f32[4,128,128]{2,1,0:T(8,128)S(1)} %convolution_add_fusion.7), channel_id=1, source_target_pairs={{0,8},{8,16},{16,24},{24,32},{32,40},{40,48},{48,56},{56,64},{64,7... | collective-permute-start | bytes 786440 | tf_op jit(solution)/shard_map/while/body/eval_jaxpr/ppermute | solution.py:14
  325.9 11.6 %collective-permute-start = (f32[4,128,128]{2,1,0:T(8,128)S(1)}, f32[4,128,128]{2,1,0:T(8,128)S(1)}, u32[]{:S(2)}, u32[]{:S(2)}) collective-permute-start(f32[4,128,128]{2,1,0:T(8,128)S(1)} %convolution_add_fusion.7), channel_id=1, source_target_pairs={{0,8},{8,16},{16,24},{24,32},{32,40},{40,48},{48,56},{56,64},{64,7... | collective-permute-start | bytes 786440 | tf_op jit(solution)/shard_map/while/body/eval_jaxpr/ppermute | solution.py:14
  338.0 10.7 %collective-permute-start = (f32[4,128,128]{2,1,0:T(8,128)S(1)}, f32[4,128,128]{2,1,0:T(8,128)S(1)}, u32[]{:S(2)}, u32[]{:S(2)}) collective-permute-start(f32[4,128,128]{2,1,0:T(8,128)S(1)} %convolution_add_fusion.7), channel_id=1, source_target_pairs={{0,8},{8,16},{16,24},{24,32},{32,40},{40,48},{48,56},{56,64},{64,7... | collective-permute-start | bytes 786440 | tf_op jit(solution)/shard_map/while/body/eval_jaxpr/ppermute | solution.py:14
  392.2 11.5 %collective-permute-start = (f32[4,128,128]{2,1,0:T(8,128)S(1)}, f32[4,128,128]{2,1,0:T(8,128)S(1)}, u32[]{:S(2)}, u32[]{:S(2)}) collective-permute-start(f32[4,128,128]{2,1,0:T(8,128)S(1)} %convolution_add_fusion.7), channel_id=1, source_target_pairs={{0,8},{8,16},{16,24},{24,32},{32,40},{40,48},{48,56},{56,64},{64,7... | collective-permute-start | bytes 786440 | tf_op jit(solution)/shard_map/while/body/eval_jaxpr/ppermute | solution.py:14
  404.1 12.7 %collective-permute-start = (f32[4,128,128]{2,1,0:T(8,128)S(1)}, f32[4,128,128]{2,1,0:T(8,128)S(1)}, u32[]{:S(2)}, u32[]{:S(2)}) collective-permute-start(f32[4,128,128]{2,1,0:T(8,128)S(1)} %convolution_add_fusion.7), channel_id=1, source_target_pairs={{0,8},{8,16},{16,24},{24,32},{32,40},{40,48},{48,56},{56,64},{64,7... | collective-permute-start | bytes 786440 | tf_op jit(solution)/shard_map/while/body/eval_jaxpr/ppermute | solution.py:14
  417.2 12.6 %collective-permute-start = (f32[4,128,128]{2,1,0:T(8,128)S(1)}, f32[4,128,128]{2,1,0:T(8,128)S(1)}, u32[]{:S(2)}, u32[]{:S(2)}) collective-permute-start(f32[4,128,128]{2,1,0:T(8,128)S(1)} %convolution_add_fusion.7), channel_id=1, source_target_pairs={{0,8},{8,16},{16,24},{24,32},{32,40},{40,48},{48,56},{56,64},{64,7... | collective-permute-start | bytes 786440 | tf_op jit(solution)/shard_map/while/body/eval_jaxpr/ppermute | solution.py:14
  430.1 11.8 %collective-permute-start = (f32[4,128,128]{2,1,0:T(8,128)S(1)}, f32[4,128,128]{2,1,0:T(8,128)S(1)}, u32[]{:S(2)}, u32[]{:S(2)}) collective-permute-start(f32[4,128,128]{2,1,0:T(8,128)S(1)} %convolution_add_fusion.7), channel_id=1, source_target_pairs={{0,8},{8,16},{16,24},{24,32},{32,40},{40,48},{48,56},{56,64},{64,7... | collective-permute-start | bytes 786440 | tf_op jit(solution)/shard_map/while/body/eval_jaxpr/ppermute | solution.py:14
  442.3 10.8 %collective-permute-start = (f32[4,128,128]{2,1,0:T(8,128)S(1)}, f32[4,128,128]{2,1,0:T(8,128)S(1)}, u32[]{:S(2)}, u32[]{:S(2)}) collective-permute-start(f32[4,128,128]{2,1,0:T(8,128)S(1)} %convolution_add_fusion.7), channel_id=1, source_target_pairs={{0,8},{8,16},{16,24},{24,32},{32,40},{40,48},{48,56},{56,64},{64,7... | collective-permute-start | bytes 786440 | tf_op jit(solution)/shard_map/while/body/eval_jaxpr/ppermute | solution.py:14
  453.5 10.4 %collective-permute-start = (f32[4,128,128]{2,1,0:T(8,128)S(1)}, f32[4,128,128]{2,1,0:T(8,128)S(1)}, u32[]{:S(2)}, u32[]{:S(2)}) collective-permute-start(f32[4,128,128]{2,1,0:T(8,128)S(1)} %convolution_add_fusion.7), channel_id=1, source_target_pairs={{0,8},{8,16},{16,24},{24,32},{32,40},{40,48},{48,56},{56,64},{64,7... | collective-permute-start | bytes 786440 | tf_op jit(solution)/shard_map/while/body/eval_jaxpr/ppermute | solution.py:14
  475.1 10.4 %collective-permute-start = (f32[4,128,128]{2,1,0:T(8,128)S(1)}, f32[4,128,128]{2,1,0:T(8,128)S(1)}, u32[]{:S(2)}, u32[]{:S(2)}) collective-permute-start(f32[4,128,128]{2,1,0:T(8,128)S(1)} %convolution_add_fusion.7), channel_id=1, source_target_pairs={{0,8},{8,16},{16,24},{24,32},{32,40},{40,48},{48,56},{56,64},{64,7... | collective-permute-start | bytes 786440 | tf_op jit(solution)/shard_map/while/body/eval_jaxpr/ppermute | solution.py:14
  496.7 11.4 %collective-permute-start = (f32[4,128,128]{2,1,0:T(8,128)S(1)}, f32[4,128,128]{2,1,0:T(8,128)S(1)}, u32[]{:S(2)}, u32[]{:S(2)}) collective-permute-start(f32[4,128,128]{2,1,0:T(8,128)S(1)} %convolution_add_fusion.7), channel_id=1, source_target_pairs={{0,8},{8,16},{16,24},{24,32},{32,40},{40,48},{48,56},{56,64},{64,7... | collective-permute-start | bytes 786440 | tf_op jit(solution)/shard_map/while/body/eval_jaxpr/ppermute | solution.py:14
  508.4 12.5 %collective-permute-start = (f32[4,128,128]{2,1,0:T(8,128)S(1)}, f32[4,128,128]{2,1,0:T(8,128)S(1)}, u32[]{:S(2)}, u32[]{:S(2)}) collective-permute-start(f32[4,128,128]{2,1,0:T(8,128)S(1)} %convolution_add_fusion.7), channel_id=1, source_target_pairs={{0,8},{8,16},{16,24},{24,32},{32,40},{40,48},{48,56},{56,64},{64,7... | collective-permute-start | bytes 786440 | tf_op jit(solution)/shard_map/while/body/eval_jaxpr/ppermute | solution.py:14
  521.4 12.7 %collective-permute-start = (f32[4,128,128]{2,1,0:T(8,128)S(1)}, f32[4,128,128]{2,1,0:T(8,128)S(1)}, u32[]{:S(2)}, u32[]{:S(2)}) collective-permute-start(f32[4,128,128]{2,1,0:T(8,128)S(1)} %convolution_add_fusion.7), channel_id=1, source_target_pairs={{0,8},{8,16},{16,24},{24,32},{32,40},{40,48},{48,56},{56,64},{64,7... | collective-permute-start | bytes 786440 | tf_op jit(solution)/shard_map/while/body/eval_jaxpr/ppermute | solution.py:14
  534.4 10.4 %collective-permute-start = (f32[4,128,128]{2,1,0:T(8,128)S(1)}, f32[4,128,128]{2,1,0:T(8,128)S(1)}, u32[]{:S(2)}, u32[]{:S(2)}) collective-permute-start(f32[4,128,128]{2,1,0:T(8,128)S(1)} %convolution_add_fusion.7), channel_id=1, source_target_pairs={{0,8},{8,16},{16,24},{24,32},{32,40},{40,48},{48,56},{56,64},{64,7... | collective-permute-start | bytes 786440 | tf_op jit(solution)/shard_map/while/body/eval_jaxpr/ppermute | solution.py:14
  (18 other events, 718.1 us)
Sparse Core Ops, SparseCore 0:
  9.2 90.7 all-gather.1
where the time goes:
time: 650 us; the launch traced here: 648 us
  waiting for transfers between devices  286 us (44%)
  other arithmetic  165 us (25%)
  matrix products  99.5 us (15%)
  starting transfers between devices  61.5 us (9%)
  blocking collectives  14.5 us (2%)
  between operations  13.7 us (2%)
    ppermute x31, waiting for transfers between devices, passed_along(): return lax.ppermute(shard, axis, pairs)  285 us
    another operation x4, other arithmetic, block_terms(): lax.linalg.triangular_solve(lower, rhs_keys, left_side=True, lower=True,...  157 us
    ppermute x31, starting transfers between devices, passed_along(): return lax.ppermute(shard, axis, pairs)  61.4 us
    dot_general x47, matrix products, matmul_heads(): jnp.einsum('hef,hfg->heg', left, right, precision=lax.Precision.HIGHEST)  26.2 us
    dot_general x8, matrix products, advance(): jnp.einsum('...ce,...ef->...cf', decayed_query, state, precision=highest)  15.5 us
    all_to_all x1, blocking collectives, on_device(): lax.all_to_all(gated, 'head', split_axis=0, concat_axis=1, tiled=True)  14.5 us
  transfers between devices with their start and end apart: 32, of which 31 were waited for; matrix products, arithmetic and copies ran while one was open for 40% of the time, Pallas kernels for 0%

commit v1 on v0

--- a/solution.py
+++ b/solution.py
@@ -115,7 +115,10 @@
     gated = (
         (core * scale * norm_gain * gate).astype(jnp.bfloat16).reshape(tok_rows, local_heads * DV)
     )
-    rows = lax.all_to_all(gated, "head", split_axis=0, concat_axis=1, tiled=True)
+    rows = jnp.concatenate(
+        lax.all_to_all(jnp.stack(jnp.split(gated, lax.axis_size("head"), axis=0)), "head", 0, 0),
+        axis=1,
+    )
     mixed = jnp.dot(
         rows,
         lax.all_gather(out_weight, "head", axis=0, tiled=True),

time: 650 us -> 649 us (level)
  no operation moved by 1% of the time
where the time goes in v1:
time: 649 us; the launch traced here: 647 us
  waiting for transfers between devices  286 us (44%)
  other arithmetic  165 us (25%)
  matrix products  99.2 us (15%)
  starting transfers between devices  61.5 us (9%)
  blocking collectives  14.5 us (2%)
  between operations  13.9 us (2%)
    ppermute x31, waiting for transfers between devices, passed_along(): return lax.ppermute(shard, axis, pairs)  285 us
    another operation x4, other arithmetic, block_terms(): lax.linalg.triangular_solve(lower, rhs_keys, left_side=True, lower=True,...  157 us
    ppermute x31, starting transfers between devices, passed_along(): return lax.ppermute(shard, axis, pairs)  61.4 us
    dot_general x47, matrix products, matmul_heads(): jnp.einsum('hef,hfg->heg', left, right, precision=lax.Precision.HIGHEST)  26 us
    dot_general x8, matrix products, advance(): jnp.einsum('...ce,...ef->...cf', decayed_query, state, precision=highest)  15.4 us
    all_to_all x1, blocking collectives, on_device(): lax.all_to_all(jnp.stack(jnp.split(gated, lax.axis_size('head'), axis=0))...  14.5 us
  transfers between devices with their start and end apart: 32, of which 31 were waited for; matrix products, arithmetic and copies ran while one was open for 40% of the time, Pallas kernels for 0%

profile of v1, /device:TPU:24, one launch (start us, length us, event | category | flops | bytes accessed | tf_op | source)
XLA Modules:
  0.0 647.2 jit_solution(7920997251120607512)
XLA Ops:
  14.5 157.3 %custom-call.5 = f32[8,4,1,64,64]{3,4,2,1,0:T(8,128)S(1)} custom-call(f32[8,4,1,64,64]{4,3,2,1,0:T(8,128)S(1)} %fusion.30), custom_call_target="InvertDiagBlocksLowerTriangular" | custom-call | tf_op jit(solution)/shard_map/triangular_solve/custom-call.1 | solution.py:42
  192.1 14.6 %while.37 = (s32[]{:T(128)}, f32[4,128,128]{2,1,0:T(8,128)S(1)}, f32[4,128,128]{2,1,0:T(8,128)S(1)}, f32[8,4,128,128]{3,2,1,0:T(8,128)S(1)}, f32[8,4,128,128]{3,2,1,0:T(8,128)}, /*index=5*/s32[]{:T(128)}, s32[]{:T(128)}) while((s32[]{:T(128)}, f32[4,128,128]{2,1,0:T(8,128)S(1)}, f32[4,128,128]{2,1,0:T(8,128)S(1)}, ...), condition=%wide.region_3.5_spmd.clone, body=%wide.region_2.0_spmd.clone.sunk | while | flops 201457664 | bytes 2884699 | solution.py:104
  206.7 359.4 %while.35 = (s32[]{:T(128)}, f32[4,128,128]{2,1,0:T(8,128)S(1)}, f32[4,128,128]{2,1,0:T(8,128)S(1)}, f32[4,128,128]{2,1,0:T(8,128)S(1)}, s32[]{:T(128)}) while((s32[]{:T(128)}, f32[4,128,128]{2,1,0:T(8,128)S(1)}, f32[4,128,128]{2,1,0:T(8,128)S(1)}, f32[4,128,128]{2,1,0:T(8,128)S(1)}, s32[]{:T(128)}) %tuple.68), condition=%wide.region_5.7_spmd, body=%wide.region_4.6_spmd.sunk | while | flops 100728832 | bytes 2097253 | solution.py:110
  211.0 10.4 %collective-permute-done = f32[4,128,128]{2,1,0:T(8,128)S(1)} collective-permute-done((f32[4,128,128]{2,1,0:T(8,128)S(1)}, f32[4,128,128]{2,1,0:T(8,128)S(1)}, u32[]{:S(2)}, u32[]{:S(2)}) %collective-permute-start) | collective-permute-done | bytes 262176 | tf_op jit(solution)/shard_map/while/body/eval_jaxpr/ppermute | solution.py:14
  223.7 9.6 %collective-permute-done = f32[4,128,128]{2,1,0:T(8,128)S(1)} collective-permute-done((f32[4,128,128]{2,1,0:T(8,128)S(1)}, f32[4,128,128]{2,1,0:T(8,128)S(1)}, u32[]{:S(2)}, u32[]{:S(2)}) %collective-permute-start) | collective-permute-done | bytes 262176 | tf_op jit(solution)/shard_map/while/body/eval_jaxpr/ppermute | solution.py:14
  235.6 8.6 %collective-permute-done = f32[4,128,128]{2,1,0:T(8,128)S(1)} collective-permute-done((f32[4,128,128]{2,1,0:T(8,128)S(1)}, f32[4,128,128]{2,1,0:T(8,128)S(1)}, u32[]{:S(2)}, u32[]{:S(2)}) %collective-permute-start) | collective-permute-done | bytes 262176 | tf_op jit(solution)/shard_map/while/body/eval_jaxpr/ppermute | solution.py:14
  246.6 8.4 %collective-permute-done = f32[4,128,128]{2,1,0:T(8,128)S(1)} collective-permute-done((f32[4,128,128]{2,1,0:T(8,128)S(1)}, f32[4,128,128]{2,1,0:T(8,128)S(1)}, u32[]{:S(2)}, u32[]{:S(2)}) %collective-permute-start) | collective-permute-done | bytes 262176 | tf_op jit(solution)/shard_map/while/body/eval_jaxpr/ppermute | solution.py:14
  278.9 8.5 %collective-permute-done = f32[4,128,128]{2,1,0:T(8,128)S(1)} collective-permute-done((f32[4,128,128]{2,1,0:T(8,128)S(1)}, f32[4,128,128]{2,1,0:T(8,128)S(1)}, u32[]{:S(2)}, u32[]{:S(2)}) %collective-permute-start) | collective-permute-done | bytes 262176 | tf_op jit(solution)/shard_map/while/body/eval_jaxpr/ppermute | solution.py:14
  289.8 9.6 %collective-permute-done = f32[4,128,128]{2,1,0:T(8,128)S(1)} collective-permute-done((f32[4,128,128]{2,1,0:T(8,128)S(1)}, f32[4,128,128]{2,1,0:T(8,128)S(1)}, u32[]{:S(2)}, u32[]{:S(2)}) %collective-permute-start) | collective-permute-done | bytes 262176 | tf_op jit(solution)/shard_map/while/body/eval_jaxpr/ppermute | solution.py:14
  301.7 10.8 %collective-permute-done = f32[4,128,128]{2,1,0:T(8,128)S(1)} collective-permute-done((f32[4,128,128]{2,1,0:T(8,128)S(1)}, f32[4,128,128]{2,1,0:T(8,128)S(1)}, u32[]{:S(2)}, u32[]{:S(2)}) %collective-permute-start) | collective-permute-done | bytes 262176 | tf_op jit(solution)/shard_map/while/body/eval_jaxpr/ppermute | solution.py:14
  314.9 10.5 %collective-permute-done = f32[4,128,128]{2,1,0:T(8,128)S(1)} collective-permute-done((f32[4,128,128]{2,1,0:T(8,128)S(1)}, f32[4,128,128]{2,1,0:T(8,128)S(1)}, u32[]{:S(2)}, u32[]{:S(2)}) %collective-permute-start) | collective-permute-done | bytes 262176 | tf_op jit(solution)/shard_map/while/body/eval_jaxpr/ppermute | solution.py:14
  327.7 9.7 %collective-permute-done = f32[4,128,128]{2,1,0:T(8,128)S(1)} collective-permute-done((f32[4,128,128]{2,1,0:T(8,128)S(1)}, f32[4,128,128]{2,1,0:T(8,128)S(1)}, u32[]{:S(2)}, u32[]{:S(2)}) %collective-permute-start) | collective-permute-done | bytes 262176 | tf_op jit(solution)/shard_map/while/body/eval_jaxpr/ppermute | solution.py:14
  339.8 8.8 %collective-permute-done = f32[4,128,128]{2,1,0:T(8,128)S(1)} collective-permute-done((f32[4,128,128]{2,1,0:T(8,128)S(1)}, f32[4,128,128]{2,1,0:T(8,128)S(1)}, u32[]{:S(2)}, u32[]{:S(2)}) %collective-permute-start) | collective-permute-done | bytes 262176 | tf_op jit(solution)/shard_map/while/body/eval_jaxpr/ppermute | solution.py:14
  394.0 9.5 %collective-permute-done = f32[4,128,128]{2,1,0:T(8,128)S(1)} collective-permute-done((f32[4,128,128]{2,1,0:T(8,128)S(1)}, f32[4,128,128]{2,1,0:T(8,128)S(1)}, u32[]{:S(2)}, u32[]{:S(2)}) %collective-permute-start) | collective-permute-done | bytes 262176 | tf_op jit(solution)/shard_map/while/body/eval_jaxpr/ppermute | solution.py:14
  405.8 10.7 %collective-permute-done = f32[4,128,128]{2,1,0:T(8,128)S(1)} collective-permute-done((f32[4,128,128]{2,1,0:T(8,128)S(1)}, f32[4,128,128]{2,1,0:T(8,128)S(1)}, u32[]{:S(2)}, u32[]{:S(2)}) %collective-permute-start) | collective-permute-done | bytes 262176 | tf_op jit(solution)/shard_map/while/body/eval_jaxpr/ppermute | solution.py:14
  418.9 10.6 %collective-permute-done = f32[4,128,128]{2,1,0:T(8,128)S(1)} collective-permute-done((f32[4,128,128]{2,1,0:T(8,128)S(1)}, f32[4,128,128]{2,1,0:T(8,128)S(1)}, u32[]{:S(2)}, u32[]{:S(2)}) %collective-permute-start) | collective-permute-done | bytes 262176 | tf_op jit(solution)/shard_map/while/body/eval_jaxpr/ppermute | solution.py:14
  431.8 9.8 %collective-permute-done = f32[4,128,128]{2,1,0:T(8,128)S(1)} collective-permute-done((f32[4,128,128]{2,1,0:T(8,128)S(1)}, f32[4,128,128]{2,1,0:T(8,128)S(1)}, u32[]{:S(2)}, u32[]{:S(2)}) %collective-permute-start) | collective-permute-done | bytes 262176 | tf_op jit(solution)/shard_map/while/body/eval_jaxpr/ppermute | solution.py:14
  444.0 8.9 %collective-permute-done = f32[4,128,128]{2,1,0:T(8,128)S(1)} collective-permute-done((f32[4,128,128]{2,1,0:T(8,128)S(1)}, f32[4,128,128]{2,1,0:T(8,128)S(1)}, u32[]{:S(2)}, u32[]{:S(2)}) %collective-permute-start) | collective-permute-done | bytes 262176 | tf_op jit(solution)/shard_map/while/body/eval_jaxpr/ppermute | solution.py:14
  498.3 9.4 %collective-permute-done = f32[4,128,128]{2,1,0:T(8,128)S(1)} collective-permute-done((f32[4,128,128]{2,1,0:T(8,128)S(1)}, f32[4,128,128]{2,1,0:T(8,128)S(1)}, u32[]{:S(2)}, u32[]{:S(2)}) %collective-permute-start) | collective-permute-done | bytes 262176 | tf_op jit(solution)/shard_map/while/body/eval_jaxpr/ppermute | solution.py:14
  510.1 10.6 %collective-permute-done = f32[4,128,128]{2,1,0:T(8,128)S(1)} collective-permute-done((f32[4,128,128]{2,1,0:T(8,128)S(1)}, f32[4,128,128]{2,1,0:T(8,128)S(1)}, u32[]{:S(2)}, u32[]{:S(2)}) %collective-permute-start) | collective-permute-done | bytes 262176 | tf_op jit(solution)/shard_map/while/body/eval_jaxpr/ppermute | solution.py:14
  523.0 10.7 %collective-permute-done = f32[4,128,128]{2,1,0:T(8,128)S(1)} collective-permute-done((f32[4,128,128]{2,1,0:T(8,128)S(1)}, f32[4,128,128]{2,1,0:T(8,128)S(1)}, u32[]{:S(2)}, u32[]{:S(2)}) %collective-permute-start) | collective-permute-done | bytes 262176 | tf_op jit(solution)/shard_map/while/body/eval_jaxpr/ppermute | solution.py:14
  566.1 46.7 %while.36 = (s32[]{:T(128)}, f32[4,128,128]{2,1,0:T(8,128)S(1)}, f32[8,4,64,128]{3,2,0,1:T(8,128)}, f32[8,4,128,128]{3,2,1,0:T(8,128)S(1)}, f32[8,4,128,128]{3,2...) while((s32[]{:T(128)}, f32[4,128,128]{2,1,0:T(8,128)S(1)}, ...), condition=%wide.region_8.10_spmd, body=%wide.region_7.9_spmd.sunk | while | flops 226623488 | bytes 3280485 | solution.py:65
  616.3 14.5 %all_to_all.5 = bf16[8,64,512]{2,1,0:T(8,128)(2,1)S(1)} all-to-all(bf16[8,64,512]{2,1,0:T(8,128)(2,1)S(1)} %constant_dynamic-update-slice_fusion), channel_id=1, replica_groups=mesh['seq'=32,'head'=8] {'head'}, dimensions={0} | all-to-all | bytes 1048576 | tf_op jit(solution)/shard_map/all_to_all | solution.py:119
  630.9 9.5 %convolution_convert_fusion = bf16[64,2048]{1,0:T(8,128)(2,1)} fusion(bf16[64,4096]{1,0:T(8,128)(2,1)S(1)} %bitcast.128, bf16[4096,2048]{1,0:T(8,128)(2,1)} %all-gather.2.cloned.1.call-done), kind=kOutput, calls=%fused_computation.31 | convolution fusion | flops 1073872896 | bytes 17563648 | tf_op jit(solution)/shard_map/dot_general | solution.py:122
  (243 shorter events, 275.3 us)
Async XLA Ops:
  6.5 624.3 %all-gather.2.cloned.1.call-start = ((), (), s32[]{:S(2)}) async-start(), calls=%async_computation.1 | async-start | bytes 18874368 | tf_op jit(solution)/shard_map/all_gather | solution.py:124
  207.1 14.2 %collective-permute-start = (f32[4,128,128]{2,1,0:T(8,128)S(1)}, f32[4,128,128]{2,1,0:T(8,128)S(1)}, u32[]{:S(2)}, u32[]{:S(2)}) collective-permute-start(f32[4,128,128]{2,1,0:T(8,128)S(1)} %convolution_add_fusion.7), channel_id=1, source_target_pairs={{0,8},{8,16},{16,24},{24,32},{32,40},{40,48},{48,56},{56,64},{64,7... | collective-permute-start | bytes 786440 | tf_op jit(solution)/shard_map/while/body/eval_jaxpr/ppermute | solution.py:14
  221.8 11.5 %collective-permute-start = (f32[4,128,128]{2,1,0:T(8,128)S(1)}, f32[4,128,128]{2,1,0:T(8,128)S(1)}, u32[]{:S(2)}, u32[]{:S(2)}) collective-permute-start(f32[4,128,128]{2,1,0:T(8,128)S(1)} %convolution_add_fusion.7), channel_id=1, source_target_pairs={{0,8},{8,16},{16,24},{24,32},{32,40},{40,48},{48,56},{56,64},{64,7... | collective-permute-start | bytes 786440 | tf_op jit(solution)/shard_map/while/body/eval_jaxpr/ppermute | solution.py:14
  233.7 10.6 %collective-permute-start = (f32[4,128,128]{2,1,0:T(8,128)S(1)}, f32[4,128,128]{2,1,0:T(8,128)S(1)}, u32[]{:S(2)}, u32[]{:S(2)}) collective-permute-start(f32[4,128,128]{2,1,0:T(8,128)S(1)} %convolution_add_fusion.7), channel_id=1, source_target_pairs={{0,8},{8,16},{16,24},{24,32},{32,40},{40,48},{48,56},{56,64},{64,7... | collective-permute-start | bytes 786440 | tf_op jit(solution)/shard_map/while/body/eval_jaxpr/ppermute | solution.py:14
  244.6 10.4 %collective-permute-start = (f32[4,128,128]{2,1,0:T(8,128)S(1)}, f32[4,128,128]{2,1,0:T(8,128)S(1)}, u32[]{:S(2)}, u32[]{:S(2)}) collective-permute-start(f32[4,128,128]{2,1,0:T(8,128)S(1)} %convolution_add_fusion.7), channel_id=1, source_target_pairs={{0,8},{8,16},{16,24},{24,32},{32,40},{40,48},{48,56},{56,64},{64,7... | collective-permute-start | bytes 786440 | tf_op jit(solution)/shard_map/while/body/eval_jaxpr/ppermute | solution.py:14
  255.4 10.4 %collective-permute-start = (f32[4,128,128]{2,1,0:T(8,128)S(1)}, f32[4,128,128]{2,1,0:T(8,128)S(1)}, u32[]{:S(2)}, u32[]{:S(2)}) collective-permute-start(f32[4,128,128]{2,1,0:T(8,128)S(1)} %convolution_add_fusion.7), channel_id=1, source_target_pairs={{0,8},{8,16},{16,24},{24,32},{32,40},{40,48},{48,56},{56,64},{64,7... | collective-permute-start | bytes 786440 | tf_op jit(solution)/shard_map/while/body/eval_jaxpr/ppermute | solution.py:14
  266.2 10.4 %collective-permute-start = (f32[4,128,128]{2,1,0:T(8,128)S(1)}, f32[4,128,128]{2,1,0:T(8,128)S(1)}, u32[]{:S(2)}, u32[]{:S(2)}) collective-permute-start(f32[4,128,128]{2,1,0:T(8,128)S(1)} %convolution_add_fusion.7), channel_id=1, source_target_pairs={{0,8},{8,16},{16,24},{24,32},{32,40},{40,48},{48,56},{56,64},{64,7... | collective-permute-start | bytes 786440 | tf_op jit(solution)/shard_map/while/body/eval_jaxpr/ppermute | solution.py:14
  277.0 10.5 %collective-permute-start = (f32[4,128,128]{2,1,0:T(8,128)S(1)}, f32[4,128,128]{2,1,0:T(8,128)S(1)}, u32[]{:S(2)}, u32[]{:S(2)}) collective-permute-start(f32[4,128,128]{2,1,0:T(8,128)S(1)} %convolution_add_fusion.7), channel_id=1, source_target_pairs={{0,8},{8,16},{16,24},{24,32},{32,40},{40,48},{48,56},{56,64},{64,7... | collective-permute-start | bytes 786440 | tf_op jit(solution)/shard_map/while/body/eval_jaxpr/ppermute | solution.py:14
  287.8 11.5 %collective-permute-start = (f32[4,128,128]{2,1,0:T(8,128)S(1)}, f32[4,128,128]{2,1,0:T(8,128)S(1)}, u32[]{:S(2)}, u32[]{:S(2)}) collective-permute-start(f32[4,128,128]{2,1,0:T(8,128)S(1)} %convolution_add_fusion.7), channel_id=1, source_target_pairs={{0,8},{8,16},{16,24},{24,32},{32,40},{40,48},{48,56},{56,64},{64,7... | collective-permute-start | bytes 786440 | tf_op jit(solution)/shard_map/while/body/eval_jaxpr/ppermute | solution.py:14
  299.8 12.8 %collective-permute-start = (f32[4,128,128]{2,1,0:T(8,128)S(1)}, f32[4,128,128]{2,1,0:T(8,128)S(1)}, u32[]{:S(2)}, u32[]{:S(2)}) collective-permute-start(f32[4,128,128]{2,1,0:T(8,128)S(1)} %convolution_add_fusion.7), channel_id=1, source_target_pairs={{0,8},{8,16},{16,24},{24,32},{32,40},{40,48},{48,56},{56,64},{64,7... | collective-permute-start | bytes 786440 | tf_op jit(solution)/shard_map/while/body/eval_jaxpr/ppermute | solution.py:14
  313.0 12.4 %collective-permute-start = (f32[4,128,128]{2,1,0:T(8,128)S(1)}, f32[4,128,128]{2,1,0:T(8,128)S(1)}, u32[]{:S(2)}, u32[]{:S(2)}) collective-permute-start(f32[4,128,128]{2,1,0:T(8,128)S(1)} %convolution_add_fusion.7), channel_id=1, source_target_pairs={{0,8},{8,16},{16,24},{24,32},{32,40},{40,48},{48,56},{56,64},{64,7... | collective-permute-start | bytes 786440 | tf_op jit(solution)/shard_map/while/body/eval_jaxpr/ppermute | solution.py:14
  325.8 11.6 %collective-permute-start = (f32[4,128,128]{2,1,0:T(8,128)S(1)}, f32[4,128,128]{2,1,0:T(8,128)S(1)}, u32[]{:S(2)}, u32[]{:S(2)}) collective-permute-start(f32[4,128,128]{2,1,0:T(8,128)S(1)} %convolution_add_fusion.7), channel_id=1, source_target_pairs={{0,8},{8,16},{16,24},{24,32},{32,40},{40,48},{48,56},{56,64},{64,7... | collective-permute-start | bytes 786440 | tf_op jit(solution)/shard_map/while/body/eval_jaxpr/ppermute | solution.py:14
  337.8 10.7 %collective-permute-start = (f32[4,128,128]{2,1,0:T(8,128)S(1)}, f32[4,128,128]{2,1,0:T(8,128)S(1)}, u32[]{:S(2)}, u32[]{:S(2)}) collective-permute-start(f32[4,128,128]{2,1,0:T(8,128)S(1)} %convolution_add_fusion.7), channel_id=1, source_target_pairs={{0,8},{8,16},{16,24},{24,32},{32,40},{40,48},{48,56},{56,64},{64,7... | collective-permute-start | bytes 786440 | tf_op jit(solution)/shard_map/while/body/eval_jaxpr/ppermute | solution.py:14
  370.5 10.4 %collective-permute-start = (f32[4,128,128]{2,1,0:T(8,128)S(1)}, f32[4,128,128]{2,1,0:T(8,128)S(1)}, u32[]{:S(2)}, u32[]{:S(2)}) collective-permute-start(f32[4,128,128]{2,1,0:T(8,128)S(1)} %convolution_add_fusion.7), channel_id=1, source_target_pairs={{0,8},{8,16},{16,24},{24,32},{32,40},{40,48},{48,56},{56,64},{64,7... | collective-permute-start | bytes 786440 | tf_op jit(solution)/shard_map/while/body/eval_jaxpr/ppermute | solution.py:14
  392.0 11.5 %collective-permute-start = (f32[4,128,128]{2,1,0:T(8,128)S(1)}, f32[4,128,128]{2,1,0:T(8,128)S(1)}, u32[]{:S(2)}, u32[]{:S(2)}) collective-permute-start(f32[4,128,128]{2,1,0:T(8,128)S(1)} %convolution_add_fusion.7), channel_id=1, source_target_pairs={{0,8},{8,16},{16,24},{24,32},{32,40},{40,48},{48,56},{56,64},{64,7... | collective-permute-start | bytes 786440 | tf_op jit(solution)/shard_map/while/body/eval_jaxpr/ppermute | solution.py:14
  403.9 12.7 %collective-permute-start = (f32[4,128,128]{2,1,0:T(8,128)S(1)}, f32[4,128,128]{2,1,0:T(8,128)S(1)}, u32[]{:S(2)}, u32[]{:S(2)}) collective-permute-start(f32[4,128,128]{2,1,0:T(8,128)S(1)} %convolution_add_fusion.7), channel_id=1, source_target_pairs={{0,8},{8,16},{16,24},{24,32},{32,40},{40,48},{48,56},{56,64},{64,7... | collective-permute-start | bytes 786440 | tf_op jit(solution)/shard_map/while/body/eval_jaxpr/ppermute | solution.py:14
  417.0 12.6 %collective-permute-start = (f32[4,128,128]{2,1,0:T(8,128)S(1)}, f32[4,128,128]{2,1,0:T(8,128)S(1)}, u32[]{:S(2)}, u32[]{:S(2)}) collective-permute-start(f32[4,128,128]{2,1,0:T(8,128)S(1)} %convolution_add_fusion.7), channel_id=1, source_target_pairs={{0,8},{8,16},{16,24},{24,32},{32,40},{40,48},{48,56},{56,64},{64,7... | collective-permute-start | bytes 786440 | tf_op jit(solution)/shard_map/while/body/eval_jaxpr/ppermute | solution.py:14
  429.9 11.8 %collective-permute-start = (f32[4,128,128]{2,1,0:T(8,128)S(1)}, f32[4,128,128]{2,1,0:T(8,128)S(1)}, u32[]{:S(2)}, u32[]{:S(2)}) collective-permute-start(f32[4,128,128]{2,1,0:T(8,128)S(1)} %convolution_add_fusion.7), channel_id=1, source_target_pairs={{0,8},{8,16},{16,24},{24,32},{32,40},{40,48},{48,56},{56,64},{64,7... | collective-permute-start | bytes 786440 | tf_op jit(solution)/shard_map/while/body/eval_jaxpr/ppermute | solution.py:14
  442.1 10.8 %collective-permute-start = (f32[4,128,128]{2,1,0:T(8,128)S(1)}, f32[4,128,128]{2,1,0:T(8,128)S(1)}, u32[]{:S(2)}, u32[]{:S(2)}) collective-permute-start(f32[4,128,128]{2,1,0:T(8,128)S(1)} %convolution_add_fusion.7), channel_id=1, source_target_pairs={{0,8},{8,16},{16,24},{24,32},{32,40},{40,48},{48,56},{56,64},{64,7... | collective-permute-start | bytes 786440 | tf_op jit(solution)/shard_map/while/body/eval_jaxpr/ppermute | solution.py:14
  453.3 10.4 %collective-permute-start = (f32[4,128,128]{2,1,0:T(8,128)S(1)}, f32[4,128,128]{2,1,0:T(8,128)S(1)}, u32[]{:S(2)}, u32[]{:S(2)}) collective-permute-start(f32[4,128,128]{2,1,0:T(8,128)S(1)} %convolution_add_fusion.7), channel_id=1, source_target_pairs={{0,8},{8,16},{16,24},{24,32},{32,40},{40,48},{48,56},{56,64},{64,7... | collective-permute-start | bytes 786440 | tf_op jit(solution)/shard_map/while/body/eval_jaxpr/ppermute | solution.py:14
  496.4 11.4 %collective-permute-start = (f32[4,128,128]{2,1,0:T(8,128)S(1)}, f32[4,128,128]{2,1,0:T(8,128)S(1)}, u32[]{:S(2)}, u32[]{:S(2)}) collective-permute-start(f32[4,128,128]{2,1,0:T(8,128)S(1)} %convolution_add_fusion.7), channel_id=1, source_target_pairs={{0,8},{8,16},{16,24},{24,32},{32,40},{40,48},{48,56},{56,64},{64,7... | collective-permute-start | bytes 786440 | tf_op jit(solution)/shard_map/while/body/eval_jaxpr/ppermute | solution.py:14
  508.2 12.6 %collective-permute-start = (f32[4,128,128]{2,1,0:T(8,128)S(1)}, f32[4,128,128]{2,1,0:T(8,128)S(1)}, u32[]{:S(2)}, u32[]{:S(2)}) collective-permute-start(f32[4,128,128]{2,1,0:T(8,128)S(1)} %convolution_add_fusion.7), channel_id=1, source_target_pairs={{0,8},{8,16},{16,24},{24,32},{32,40},{40,48},{48,56},{56,64},{64,7... | collective-permute-start | bytes 786440 | tf_op jit(solution)/shard_map/while/body/eval_jaxpr/ppermute | solution.py:14
  521.1 12.7 %collective-permute-start = (f32[4,128,128]{2,1,0:T(8,128)S(1)}, f32[4,128,128]{2,1,0:T(8,128)S(1)}, u32[]{:S(2)}, u32[]{:S(2)}) collective-permute-start(f32[4,128,128]{2,1,0:T(8,128)S(1)} %convolution_add_fusion.7), channel_id=1, source_target_pairs={{0,8},{8,16},{16,24},{24,32},{32,40},{40,48},{48,56},{56,64},{64,7... | collective-permute-start | bytes 786440 | tf_op jit(solution)/shard_map/while/body/eval_jaxpr/ppermute | solution.py:14
  534.2 10.4 %collective-permute-start = (f32[4,128,128]{2,1,0:T(8,128)S(1)}, f32[4,128,128]{2,1,0:T(8,128)S(1)}, u32[]{:S(2)}, u32[]{:S(2)}) collective-permute-start(f32[4,128,128]{2,1,0:T(8,128)S(1)} %convolution_add_fusion.7), channel_id=1, source_target_pairs={{0,8},{8,16},{16,24},{24,32},{32,40},{40,48},{48,56},{56,64},{64,7... | collective-permute-start | bytes 786440 | tf_op jit(solution)/shard_map/while/body/eval_jaxpr/ppermute | solution.py:14
  (18 other events, 158.4 us)
Sparse Core Ops, SparseCore 0:
  9.2 90.6 all-gather.1
